TPU v7x, 32 devices: a whole 2x2x4 slice. The times are simulated.
32 devices in a mesh: blk: 2 (over y), uly: 16 (over z, x, core).
Axes of the slice: x: 2, y: 2, z: 4, core: 2. Of those that a mesh axis runs over, the one named last changes fastest.
Arguments:
- queries: bfloat16 [4096, 2048], P(('blk', 'uly')), may hold values from -8 to 8
- keys: bfloat16 [4096, 2048], P(('blk', 'uly')), may hold values from -8 to 8
- values: bfloat16 [4096, 2048], P(('blk', 'uly')), may hold values from -6 to 6
- grad_out: bfloat16 [4096, 2048], P(('blk', 'uly')), may hold values from -6 to 6
- doc_start: int32 [32], replicated, may hold values from 0 to 3968, as said below
Outputs:
- grad_queries: bfloat16 [4096, 2048], P(('blk', 'uly'))
- grad_keys: bfloat16 [4096, 2048], P(('blk', 'uly'))
- grad_values: bfloat16 [4096, 2048], P(('blk', 'uly'))
Inputs may be any that keep to these rules, and one draw needn't show every extreme that they name: `doc_start`: each entry is the first position of its block's document, so documents are runs of whole blocks; no document is longer than 8 blocks and one is exactly 8; a document crosses every boundary between groups of 2048 positions and starts at most 7 blocks before it, at one boundary exactly 7; the last block starts a document.
All inputs are finite; a program needn't handle non-finite values.
Results may differ from a plain program's by a relative error of at most 0.0051.
Values may be sent and summed in bfloat16 or wider, within the bound.
A program may use at most 64 MiB of HBM per device.

v0:
```python
import math
import jax
import jax.numpy as jnp
from jax import lax
from jax.sharding import PartitionSpec as P

BLOCK = 128
MAXB = 8


def passed_along(array, axis, by):
    devices = lax.axis_size(axis)
    pairs = [(i, i + by) for i in range(devices) if 0 <= i + by < devices]
    return lax.ppermute(array, axis, pairs)


def body(queries, keys, values, grad_out, doc_start):
    q_all, k_all, v_all, d_all = (
        lax.all_to_all(queries, "uly", split_axis=1, concat_axis=0, tiled=True),
        lax.all_to_all(keys, "uly", split_axis=1, concat_axis=0, tiled=True),
        lax.all_to_all(values, "uly", split_axis=1, concat_axis=0, tiled=True),
        lax.all_to_all(grad_out, "uly", split_axis=1, concat_axis=0, tiled=True),
    )
    group_rows, width = q_all.shape
    tile = 4 * BLOCK
    fetch_rows = (MAXB - 1) * BLOCK
    lead_tiles = -(-fetch_rows // tile)
    lead_rows = lead_tiles * tile
    pad_rows = lead_rows - fetch_rows
    lead_blocks = lead_rows // BLOCK
    local_blocks = group_rows // BLOCK
    ext_rows = lead_rows + group_rows
    group = lax.axis_index("blk")
    scale = 1.0 / math.sqrt(width)
    split_at = group_rows - fetch_rows
    tail_k = k_all[split_at:]
    tail_v = v_all[split_at:]
    far_k, far_v = passed_along((tail_k, tail_v), "blk", 1)
    blank = jnp.zeros((pad_rows, width), jnp.bfloat16)
    ext_k = jnp.concatenate([blank, far_k, k_all], 0)
    ext_v = jnp.concatenate([blank, far_v, v_all], 0)
    padded_docs = jnp.concatenate([jnp.full((lead_blocks,), -1, jnp.int32), doc_start], 0)
    block_doc = lax.dynamic_slice_in_dim(
        padded_docs, group * local_blocks, lead_blocks + local_blocks, 0
    )
    block_doc = jnp.where(jnp.arange(lead_blocks + local_blocks) < pad_rows // BLOCK, -1, block_doc)
    key_doc = jnp.repeat(block_doc, BLOCK)
    first_pos = (group * local_blocks - lead_blocks) * BLOCK
    key_pos = first_pos + jnp.arange(ext_rows, dtype=jnp.int32)
    query_doc = key_doc[lead_rows:]
    query_pos = key_pos[lead_rows:]

    def query_tile(t, carry):
        dq_all, dk_ext, dv_ext, lse_all, delta_all = carry
        q_start = t * tile
        q_rows = lax.dynamic_slice_in_dim(q_all, q_start, tile, 0)
        d_rows = lax.dynamic_slice_in_dim(d_all, q_start, tile, 0)
        q_doc = lax.dynamic_slice_in_dim(query_doc, q_start, tile, 0)
        q_pos = lax.dynamic_slice_in_dim(query_pos, q_start, tile, 0)
        lower = (q_doc[0] - first_pos) // tile
        upper = t + lead_tiles + 1

        def scores(j):
            k_start = j * tile
            k_rows = lax.dynamic_slice_in_dim(ext_k, k_start, tile, 0)
            v_rows = lax.dynamic_slice_in_dim(ext_v, k_start, tile, 0)
            k_doc = lax.dynamic_slice_in_dim(key_doc, k_start, tile, 0)
            k_pos = lax.dynamic_slice_in_dim(key_pos, k_start, tile, 0)
            allowed = (q_doc[:, None] == k_doc[None, :]) & (k_pos[None, :] <= q_pos[:, None])
            score = (
                jnp.einsum("qd,kd->qk", q_rows, k_rows, preferred_element_type=jnp.float32) * scale
            )
            score = jnp.where(allowed, score, -1e30)
            dprob = jnp.einsum("qd,kd->qk", d_rows, v_rows, preferred_element_type=jnp.float32)
            return (k_rows, score, allowed, dprob)

        def first_pass(j, stats):
            top, total, cross = stats
            k_rows, score, allowed, dprob = scores(j)
            new_top = jnp.maximum(top, jnp.max(score, axis=1))
            fade = jnp.exp(top - new_top)
            weight = jnp.where(allowed, jnp.exp(score - new_top[:, None]), 0.0)
            return (
                new_top,
                total * fade + jnp.sum(weight, axis=1),
                cross * fade + jnp.sum(weight * dprob, axis=1),
            )

        start_stats = (
            jnp.full((tile,), -1e30, jnp.float32),
            jnp.zeros((tile,), jnp.float32),
            jnp.zeros((tile,), jnp.float32),
        )
        top, total, cross = lax.fori_loop(lower, upper, first_pass, start_stats)
        lse = top + jnp.log(total)
        delta = cross / total

        def tile_terms(j):
            k_rows, score, allowed, dprob = scores(j)
            prob = jnp.where(allowed, jnp.exp(score - lse[:, None]), 0.0)
            dscore = (prob * (dprob - delta[:, None]) * scale).astype(jnp.bfloat16)
            prob_low = prob.astype(jnp.bfloat16)
            return (k_rows, dscore, prob_low)

        def full_pass(j, acc):
            dq_part, dk_acc, dv_acc = acc
            k_rows, dscore, prob_low = tile_terms(j)
            dq_part = dq_part + jnp.einsum(
                "qk,kd->qd", dscore, k_rows, preferred_element_type=jnp.float32
            )
            k_start = j * tile
            dk_acc = lax.dynamic_update_slice_in_dim(
                dk_acc,
                lax.dynamic_slice_in_dim(dk_acc, k_start, tile, 0)
                + jnp.einsum("qk,qd->kd", dscore, q_rows, preferred_element_type=jnp.float32),
                k_start,
                0,
            )
            dv_acc = lax.dynamic_update_slice_in_dim(
                dv_acc,
                lax.dynamic_slice_in_dim(dv_acc, k_start, tile, 0)
                + jnp.einsum("qk,qd->kd", prob_low, d_rows, preferred_element_type=jnp.float32),
                k_start,
                0,
            )
            return (dq_part, dk_acc, dv_acc)

        start_acc = (jnp.zeros((tile, width), jnp.float32), dk_ext, dv_ext)
        dq_part, dk_ext, dv_ext = lax.fori_loop(lower, upper, full_pass, start_acc)
        dq_all = lax.dynamic_update_slice_in_dim(dq_all, dq_part.astype(jnp.bfloat16), q_start, 0)
        lse_all = lax.dynamic_update_slice_in_dim(lse_all, lse, q_start, 0)
        delta_all = lax.dynamic_update_slice_in_dim(delta_all, delta, q_start, 0)
        return (dq_all, dk_ext, dv_ext, lse_all, delta_all)

    start_carry = (
        jnp.zeros((group_rows, width), jnp.bfloat16),
        jnp.zeros((ext_rows, width), jnp.float32),
        jnp.zeros((ext_rows, width), jnp.float32),
        jnp.zeros((group_rows,), jnp.float32),
        jnp.zeros((group_rows,), jnp.float32),
    )
    dq_all, dk_ext, dv_ext, lse_all, delta_all = lax.fori_loop(
        0, group_rows // tile, query_tile, start_carry
    )
    near_k = dk_ext[pad_rows:lead_rows]
    near_v = dv_ext[pad_rows:lead_rows]
    back_k, back_v = (
        passed_along(near_k.astype(jnp.bfloat16), "blk", -1).astype(near_k.dtype),
        passed_along(near_v.astype(jnp.bfloat16), "blk", -1).astype(near_v.dtype),
    )
    own_k = dk_ext[lead_rows:]
    own_v = dv_ext[lead_rows:]
    own_k = jnp.concatenate([own_k[:split_at], own_k[split_at:] + back_k], 0).astype(jnp.bfloat16)
    own_v = jnp.concatenate([own_v[:split_at], own_v[split_at:] + back_v], 0).astype(jnp.bfloat16)
    grad_q, grad_k, grad_v = (
        lax.all_to_all(dq_all, "uly", split_axis=0, concat_axis=1, tiled=True),
        lax.all_to_all(own_k, "uly", split_axis=0, concat_axis=1, tiled=True),
        lax.all_to_all(own_v, "uly", split_axis=0, concat_axis=1, tiled=True),
    )
    return (grad_q, grad_k, grad_v)


def solution(mesh):
    return jax.shard_map(
        body,
        mesh=mesh,
        in_specs=(
            P(("blk", "uly"), None),
            P(("blk", "uly"), None),
            P(("blk", "uly"), None),
            P(("blk", "uly"), None),
            P(),
        ),
        out_specs=(P(("blk", "uly"), None), P(("blk", "uly"), None), P(("blk", "uly"), None)),
        check_vma=False,
    )
```

profile of v0, /device:TPU:0, one launch (start us, length us, event | category | flops | bytes accessed | tf_op | source)
XLA Modules:
  0.0 212.2 jit_solution(1656074827154237378)
XLA Ops:
  2.6 7.5 %all-to-all-start.2 = ((bf16[128,16,128]{2,0,1:T(8,128)(2,1)}), bf16[128,16,128]{2,0,1:T(8,128)(2,1)S(1)}, u32[]{:S(2)}, u32[]{:S(2)}) async-start(bf16[128,16,128]{2,0,1:T(8,128)(2,1)} %copy_bitcast_fusion.1), calls=%async_computation.2 | async-start | bytes 1048576 | tf_op jit(solution)/shard_map/all_to_all | solution.py:20
  11.1 13.3 %all-to-all-done.2 = bf16[128,16,128]{2,0,1:T(8,128)(2,1)S(1)} async-done(((bf16[128,16,128]{2,0,1:T(8,128)(2,1)}), bf16[128,16,128]{2,0,1:T(8,128)(2,1)S(1)}, u32[]{:S(2)}, u32[]{:S(2)}) %all-to-all-start.2) | async-done | bytes 524320 | tf_op jit(solution)/shard_map/all_to_all | solution.py:20
  24.4 4.2 %all-to-all-start.3 = ((bf16[128,16,128]{2,0,1:T(8,128)(2,1)}), bf16[128,16,128]{2,0,1:T(8,128)(2,1)S(1)}, u32[]{:S(2)}, u32[]{:S(2)}) async-start(bf16[128,16,128]{2,0,1:T(8,128)(2,1)} %copy_bitcast_fusion), calls=%async_computation.3 | async-start | bytes 1048576 | tf_op jit(solution)/shard_map/all_to_all | solution.py:21
  29.5 13.3 %all-to-all-done.3 = bf16[128,16,128]{2,0,1:T(8,128)(2,1)S(1)} async-done(((bf16[128,16,128]{2,0,1:T(8,128)(2,1)}), bf16[128,16,128]{2,0,1:T(8,128)(2,1)S(1)}, u32[]{:S(2)}, u32[]{:S(2)}) %all-to-all-start.3) | async-done | bytes 524320 | tf_op jit(solution)/shard_map/all_to_all | solution.py:21
  42.8 4.2 %all-to-all-start = ((bf16[128,16,128]{2,0,1:T(8,128)(2,1)}), bf16[128,16,128]{2,0,1:T(8,128)(2,1)S(1)}, u32[]{:S(2)}, u32[]{:S(2)}) async-start(bf16[128,16,128]{2,0,1:T(8,128)(2,1)} %copy_bitcast_fusion.3), calls=%async_computation | async-start | bytes 1048576 | tf_op jit(solution)/shard_map/all_to_all | solution.py:19
  48.0 3.4 %collective-permute-start = (bf16[896,128]{1,0:T(8,128)(2,1)S(1)}, bf16[896,128]{1,0:T(8,128)(2,1)S(1)}, u32[]{:S(2)}, u32[]{:S(2)}) collective-permute-start(bf16[896,128]{1,0:T(8,128)(2,1)S(1)} %bitcast.122), channel_id=1, source_target_pairs={{0,16},{1,17},{2,18},{3,19},{4,20},{5,21},{6,22},{7,23},{8,24},{9,... | collective-permute-start | bytes 688136 | tf_op jit(solution)/shard_map/ppermute | solution.py:14
  51.5 1.3 collective-permute-start.1
  52.8 8.5 %all-to-all-done = bf16[128,16,128]{2,0,1:T(8,128)(2,1)S(1)} async-done(((bf16[128,16,128]{2,0,1:T(8,128)(2,1)}), bf16[128,16,128]{2,0,1:T(8,128)(2,1)S(1)}, u32[]{:S(2)}, u32[]{:S(2)}) %all-to-all-start) | async-done | bytes 524320 | tf_op jit(solution)/shard_map/all_to_all | solution.py:19
  61.3 4.2 %all-to-all-start.1 = ((bf16[128,16,128]{2,0,1:T(8,128)(2,1)}), bf16[128,16,128]{2,0,1:T(8,128)(2,1)}, u32[]{:S(2)}, u32[]{:S(2)}) async-start(bf16[128,16,128]{2,0,1:T(8,128)(2,1)} %copy_bitcast_fusion.2), calls=%async_computation.1 | async-start | bytes 1048576 | tf_op jit(solution)/shard_map/all_to_all | solution.py:22
  65.8 4.3 %pad_maximum_fusion.1 = (bf16[3072,128]{1,0:T(8,128)(2,1)S(1)}, bf16[3072,128]{1,0:T(8,128)(2,1)}) fusion(bf16[2048,128]{1,0:T(8,128)(2,1)S(1)} %bitcast.116, bf16[896,128]{1,0:T(8,128)(2,1)S(1)} %collective-permute-done.1, bf16[3072]{0:T(1024)(128)(2,1)S(1)} %pad.8.clone, bf16[2048,128]{1,0:T(8,128)(2,1)S(1)} %bitcast.114, ...), kind=kLoop, calls=%fused_computation.48 | loop fusion | flops 4325376 | bytes 3086336 | tf_op jit(solution)/shard_map/concatenate | solution.py:41
  70.1 9.8 %all-to-all-done.1 = bf16[128,16,128]{2,0,1:T(8,128)(2,1)} async-done(((bf16[128,16,128]{2,0,1:T(8,128)(2,1)}), bf16[128,16,128]{2,0,1:T(8,128)(2,1)}, u32[]{:S(2)}, u32[]{:S(2)}) %all-to-all-start.1) | async-done | bytes 524320 | tf_op jit(solution)/shard_map/all_to_all | solution.py:22
  82.1 58.6 %while.115 = (s32[]{:T(128)}, bf16[2048,128]{1,0:T(8,128)(2,1)}, f32[3072,128]{1,0:T(8,128)}, f32[3072,128]{1,0:T(8,128)S(1)}, s32[2048]{0:T(1024)S(1)}, /*index...) while((s32[]{:T(128)}, bf16[2048,128]{1,0:T(8,128)(2,1)}, ...), condition=%wide.region_8.9_spmd.clone.clone, body=%wide.region_0.8_spmd.clone.clone.sunk | while | flops 478156288 | bytes 12199279 | solution.py:142
  84.5 2.3 %while.116 = (s32[]{:T(128)}, f32[512]{0:T(512)S(1)}, f32[512]{0:T(512)S(1)}, f32[512]{0:T(512)S(1)}, s32[]{:T(128)}, /*index=5*/s32[512]{0:T(512)S(1)}, s32[307...) while((s32[]{:T(128)}, f32[512]{0:T(512)S(1)}, ...), condition=%wide.region_5.5_spmd, body=%wide.region_1.4_spmd.sunk | while | flops 139200000 | bytes 3739867 | solution.py:94
  84.7 1.3 fusion.70
  86.8 5.4 %while.117 = (s32[]{:T(128)}, f32[512,128]{1,0:T(8,128)S(1)}, f32[3072,128]{1,0:T(8,128)}, f32[3072,128]{1,0:T(8,128)S(1)}, s32[]{:T(128)}, /*index=5*/s32[512]{...) while((s32[]{:T(128)}, f32[512,128]{1,0:T(8,128)S(1)}, ...), condition=%wide.region_7.7_spmd, body=%wide.region_6.6_spmd.sunk | while | flops 338886656 | bytes 7229687 | solution.py:129
  87.0 1.4 fusion.83
  90.3 1.9 fusion.85
  95.4 4.5 %while.116 = (s32[]{:T(128)}, f32[512]{0:T(512)S(1)}, f32[512]{0:T(512)S(1)}, f32[512]{0:T(512)S(1)}, s32[]{:T(128)}, /*index=5*/s32[512]{0:T(512)S(1)}, s32[307...) while((s32[]{:T(128)}, f32[512]{0:T(512)S(1)}, ...), condition=%wide.region_5.5_spmd, body=%wide.region_1.4_spmd.sunk | while | flops 139200000 | bytes 3739867 | solution.py:94
  95.5 1.3 fusion.70
  97.8 1.3 fusion.70
  100.0 10.8 %while.117 = (s32[]{:T(128)}, f32[512,128]{1,0:T(8,128)S(1)}, f32[3072,128]{1,0:T(8,128)}, f32[3072,128]{1,0:T(8,128)S(1)}, s32[]{:T(128)}, /*index=5*/s32[512]{...) while((s32[]{:T(128)}, f32[512,128]{1,0:T(8,128)S(1)}, ...), condition=%wide.region_7.7_spmd, body=%wide.region_6.6_spmd.sunk | while | flops 338886656 | bytes 7229687 | solution.py:129
  100.1 1.4 fusion.83
  101.8 1.3 convolution_add_fusion.4
  103.4 1.9 fusion.85
  105.5 1.4 fusion.83
  108.8 2.0 fusion.85
  113.8 2.3 %while.116 = (s32[]{:T(128)}, f32[512]{0:T(512)S(1)}, f32[512]{0:T(512)S(1)}, f32[512]{0:T(512)S(1)}, s32[]{:T(128)}, /*index=5*/s32[512]{0:T(512)S(1)}, s32[307...) while((s32[]{:T(128)}, f32[512]{0:T(512)S(1)}, ...), condition=%wide.region_5.5_spmd, body=%wide.region_1.4_spmd.sunk | while | flops 139200000 | bytes 3739867 | solution.py:94
  114.0 1.3 fusion.70
  116.1 5.4 %while.117 = (s32[]{:T(128)}, f32[512,128]{1,0:T(8,128)S(1)}, f32[3072,128]{1,0:T(8,128)}, f32[3072,128]{1,0:T(8,128)S(1)}, s32[]{:T(128)}, /*index=5*/s32[512]{...) while((s32[]{:T(128)}, f32[512,128]{1,0:T(8,128)S(1)}, ...), condition=%wide.region_7.7_spmd, body=%wide.region_6.6_spmd.sunk | while | flops 338886656 | bytes 7229687 | solution.py:129
  116.3 1.4 fusion.83
  119.6 1.9 fusion.85
  124.6 4.5 %while.116 = (s32[]{:T(128)}, f32[512]{0:T(512)S(1)}, f32[512]{0:T(512)S(1)}, f32[512]{0:T(512)S(1)}, s32[]{:T(128)}, /*index=5*/s32[512]{0:T(512)S(1)}, s32[307...) while((s32[]{:T(128)}, f32[512]{0:T(512)S(1)}, ...), condition=%wide.region_5.5_spmd, body=%wide.region_1.4_spmd.sunk | while | flops 139200000 | bytes 3739867 | solution.py:94
  124.8 1.3 fusion.70
  127.1 1.3 fusion.70
  129.2 10.8 %while.117 = (s32[]{:T(128)}, f32[512,128]{1,0:T(8,128)S(1)}, f32[3072,128]{1,0:T(8,128)}, f32[3072,128]{1,0:T(8,128)S(1)}, s32[]{:T(128)}, /*index=5*/s32[512]{...) while((s32[]{:T(128)}, f32[512,128]{1,0:T(8,128)S(1)}, ...), condition=%wide.region_7.7_spmd, body=%wide.region_6.6_spmd.sunk | while | flops 338886656 | bytes 7229687 | solution.py:129
  129.4 1.4 fusion.83
  132.7 1.9 fusion.85
  134.8 1.4 fusion.83
  138.0 1.9 fusion.85
  140.7 4.2 %all-to-all-start.4 = ((bf16[16,128,128]{2,1,0:T(8,128)(2,1)}), bf16[16,128,128]{2,1,0:T(8,128)(2,1)S(1)}, u32[]{:S(2)}, u32[]{:S(2)}) async-start(bf16[16,128,128]{2,1,0:T(8,128)(2,1)} %bitcast.118), calls=%async_computation.4 | async-start | bytes 1048576 | tf_op jit(solution)/shard_map/all_to_all | solution.py:156
  144.9 1.3 collective-permute-start.3
  146.3 22.9 %collective-permute-done.3 = bf16[896,128]{1,0:T(8,128)(2,1)S(1)} collective-permute-done((bf16[896,128]{1,0:T(8,128)(2,1)S(1)}, bf16[896,128]{1,0:T(8,128)(2,1)S(1)}, u32[]{:S(2)}, u32[]{:S(2)}) %collective-permute-start.3) | collective-permute-done | bytes 229408 | tf_op jit(solution)/shard_map/ppermute | solution.py:14
  170.1 5.7 %all-to-all-start.6 = ((bf16[16,128,128]{2,1,0:T(8,128)(2,1)}), bf16[16,128,128]{2,1,0:T(8,128)(2,1)S(1)}, u32[]{:S(2)}, u32[]{:S(2)}) async-start(bf16[16,128,128]{2,1,0:T(8,128)(2,1)} %bitcast.21), calls=%async_computation.6 | async-start | bytes 1048576 | tf_op jit(solution)/shard_map/all_to_all | solution.py:158
  175.8 1.5 convert.16
  177.3 1.3 collective-permute-start.2
  178.6 10.4 %collective-permute-done.2 = bf16[896,128]{1,0:T(8,128)(2,1)S(1)} collective-permute-done((bf16[896,128]{1,0:T(8,128)(2,1)S(1)}, bf16[896,128]{1,0:T(8,128)(2,1)S(1)}, u32[]{:S(2)}, u32[]{:S(2)}) %collective-permute-start.2) | collective-permute-done | bytes 229408 | tf_op jit(solution)/shard_map/ppermute | solution.py:14
  190.9 5.7 %all-to-all-start.5 = ((bf16[16,128,128]{2,1,0:T(8,128)(2,1)}), bf16[16,128,128]{2,1,0:T(8,128)(2,1)S(1)}, u32[]{:S(2)}, u32[]{:S(2)}) async-start(bf16[16,128,128]{2,1,0:T(8,128)(2,1)} %bitcast.18), calls=%async_computation.5 | async-start | bytes 1048576 | tf_op jit(solution)/shard_map/all_to_all | solution.py:157
  199.2 11.7 %all-to-all-done.5 = bf16[16,128,128]{2,1,0:T(8,128)(2,1)S(1)} async-done(((bf16[16,128,128]{2,1,0:T(8,128)(2,1)}), bf16[16,128,128]{2,1,0:T(8,128)(2,1)S(1)}, u32[]{:S(2)}, u32[]{:S(2)}) %all-to-all-start.5) | async-done | bytes 524320 | tf_op jit(solution)/shard_map/all_to_all | solution.py:157
  (165 shorter events, 40.3 us)
Async XLA Ops:
  0.6 1.0 copy-start
  0.6 9.5 %copy-start.2 = (bf16[128,2048]{1,0:T(8,128)(2,1)S(1)}, bf16[128,2048]{1,0:T(8,128)(2,1)}, u32[]{:S(2)}) copy-start(bf16[128,2048]{1,0:T(8,128)(2,1)} %param.13) | copy-start | bytes 1572868
  2.6 26.0 %copy-start.3 = (bf16[128,2048]{1,0:T(8,128)(2,1)S(1)}, bf16[128,2048]{1,0:T(8,128)(2,1)}, u32[]{:S(2)}) copy-start(bf16[128,2048]{1,0:T(8,128)(2,1)} %param.11) | copy-start | bytes 1572868
  2.6 21.8 %all-to-all-start.2 = ((bf16[128,16,128]{2,0,1:T(8,128)(2,1)}), bf16[128,16,128]{2,0,1:T(8,128)(2,1)S(1)}, u32[]{:S(2)}, u32[]{:S(2)}) async-start(bf16[128,16,128]{2,0,1:T(8,128)(2,1)} %copy_bitcast_fusion.1), calls=%async_computation.2 | async-start | bytes 1048576 | tf_op jit(solution)/shard_map/all_to_all | solution.py:20
  11.1 36.0 %copy-start.4 = (bf16[128,2048]{1,0:T(8,128)(2,1)S(1)}, bf16[128,2048]{1,0:T(8,128)(2,1)}, u32[]{:S(2)}) copy-start(bf16[128,2048]{1,0:T(8,128)(2,1)} %param.14) | copy-start | bytes 1572868
  24.4 18.4 %all-to-all-start.3 = ((bf16[128,16,128]{2,0,1:T(8,128)(2,1)}), bf16[128,16,128]{2,0,1:T(8,128)(2,1)S(1)}, u32[]{:S(2)}, u32[]{:S(2)}) async-start(bf16[128,16,128]{2,0,1:T(8,128)(2,1)} %copy_bitcast_fusion), calls=%async_computation.3 | async-start | bytes 1048576 | tf_op jit(solution)/shard_map/all_to_all | solution.py:21
  42.8 18.4 %all-to-all-start = ((bf16[128,16,128]{2,0,1:T(8,128)(2,1)}), bf16[128,16,128]{2,0,1:T(8,128)(2,1)S(1)}, u32[]{:S(2)}, u32[]{:S(2)}) async-start(bf16[128,16,128]{2,0,1:T(8,128)(2,1)} %copy_bitcast_fusion.3), calls=%async_computation | async-start | bytes 1048576 | tf_op jit(solution)/shard_map/all_to_all | solution.py:19
  47.0 18.5 %copy-start.5 = (s32[32]{0:T(128)S(1)}, s32[32]{0:T(128)}, u32[]{:S(2)}) copy-start(s32[32]{0:T(128)} %param.15) | copy-start | bytes 388
  48.0 17.8 %collective-permute-start = (bf16[896,128]{1,0:T(8,128)(2,1)S(1)}, bf16[896,128]{1,0:T(8,128)(2,1)S(1)}, u32[]{:S(2)}, u32[]{:S(2)}) collective-permute-start(bf16[896,128]{1,0:T(8,128)(2,1)S(1)} %bitcast.122), channel_id=1, source_target_pairs={{0,16},{1,17},{2,18},{3,19},{4,20},{5,21},{6,22},{7,23},{8,24},{9,... | collective-permute-start | bytes 688136 | tf_op jit(solution)/shard_map/ppermute | solution.py:14
  51.5 14.3 %collective-permute-start.1 = (bf16[896,128]{1,0:T(8,128)(2,1)S(1)}, bf16[896,128]{1,0:T(8,128)(2,1)S(1)}, u32[]{:S(2)}, u32[]{:S(2)}) collective-permute-start(bf16[896,128]{1,0:T(8,128)(2,1)S(1)} %bitcast.123), channel_id=1, source_target_pairs={{0,16},{1,17},{2,18},{3,19},{4,20},{5,21},{6,22},{7,23},{8,24},{9,... | collective-permute-start | bytes 688136 | tf_op jit(solution)/shard_map/ppermute | solution.py:14
  61.3 8.8 %copy-start.1 = (bf16[128,16,128]{2,0,1:T(8,128)(2,1)}, bf16[128,16,128]{2,0,1:T(8,128)(2,1)S(1)}, u32[]{:S(2)}) copy-start(bf16[128,16,128]{2,0,1:T(8,128)(2,1)S(1)} %all-to-all-done) | copy-start | bytes 1572868
  61.3 18.5 %all-to-all-start.1 = ((bf16[128,16,128]{2,0,1:T(8,128)(2,1)}), bf16[128,16,128]{2,0,1:T(8,128)(2,1)}, u32[]{:S(2)}, u32[]{:S(2)}) async-start(bf16[128,16,128]{2,0,1:T(8,128)(2,1)} %copy_bitcast_fusion.2), calls=%async_computation.1 | async-start | bytes 1048576 | tf_op jit(solution)/shard_map/all_to_all | solution.py:22
  140.7 29.4 %all-to-all-start.4 = ((bf16[16,128,128]{2,1,0:T(8,128)(2,1)}), bf16[16,128,128]{2,1,0:T(8,128)(2,1)S(1)}, u32[]{:S(2)}, u32[]{:S(2)}) async-start(bf16[16,128,128]{2,1,0:T(8,128)(2,1)} %bitcast.118), calls=%async_computation.4 | async-start | bytes 1048576 | tf_op jit(solution)/shard_map/all_to_all | solution.py:156
  144.9 24.2 %collective-permute-start.3 = (bf16[896,128]{1,0:T(8,128)(2,1)S(1)}, bf16[896,128]{1,0:T(8,128)(2,1)S(1)}, u32[]{:S(2)}, u32[]{:S(2)}) collective-permute-start(bf16[896,128]{1,0:T(8,128)(2,1)S(1)} %slice.80), channel_id=1, source_target_pairs={{16,0},{17,1},{18,2},{19,3},{20,4},{21,5},{22,6},{23,7},{24,8},{25... | collective-permute-start | bytes 688136 | tf_op jit(solution)/shard_map/ppermute | solution.py:14
  170.1 20.9 %all-to-all-start.6 = ((bf16[16,128,128]{2,1,0:T(8,128)(2,1)}), bf16[16,128,128]{2,1,0:T(8,128)(2,1)S(1)}, u32[]{:S(2)}, u32[]{:S(2)}) async-start(bf16[16,128,128]{2,1,0:T(8,128)(2,1)} %bitcast.21), calls=%async_computation.6 | async-start | bytes 1048576 | tf_op jit(solution)/shard_map/all_to_all | solution.py:158
  177.3 11.7 %collective-permute-start.2 = (bf16[896,128]{1,0:T(8,128)(2,1)S(1)}, bf16[896,128]{1,0:T(8,128)(2,1)S(1)}, u32[]{:S(2)}, u32[]{:S(2)}) collective-permute-start(bf16[896,128]{1,0:T(8,128)(2,1)S(1)} %slice.78), channel_id=1, source_target_pairs={{16,0},{17,1},{18,2},{19,3},{20,4},{21,5},{22,6},{23,7},{24,8},{25... | collective-permute-start | bytes 688136 | tf_op jit(solution)/shard_map/ppermute | solution.py:14
  190.9 20.0 %all-to-all-start.5 = ((bf16[16,128,128]{2,1,0:T(8,128)(2,1)}), bf16[16,128,128]{2,1,0:T(8,128)(2,1)S(1)}, u32[]{:S(2)}, u32[]{:S(2)}) async-start(bf16[16,128,128]{2,1,0:T(8,128)(2,1)} %bitcast.18), calls=%async_computation.5 | async-start | bytes 1048576 | tf_op jit(solution)/shard_map/all_to_all | solution.py:157
where the time goes:
time: 214 us; the launch traced here: 212 us
  waiting for transfers between devices  89.9 us (42%)
  starting transfers between devices  43 us (20%)
  matrix products  41.5 us (19%)
  local copies, waits for them, and re-layouts  20 us (9%)
  other arithmetic  13.4 us (6%)
  loops' own time  3.49 us (2%)
    ppermute x4, waiting for transfers between devices, passed_along(): return lax.ppermute(array, axis, pairs)  33.3 us
    dot_general x12, matrix products, scores(): jnp.einsum('qd,kd->qk', q_rows, k_rows, preferred_element_type=jnp.float32)  15.9 us
    all_to_all x1, waiting for transfers between devices, body(): lax.all_to_all(values, 'uly', split_axis=1, concat_axis=0, tiled=True)  13.3 us
    all_to_all x1, waiting for transfers between devices, body(): lax.all_to_all(keys, 'uly', split_axis=1, concat_axis=0, tiled=True)  13.3 us
    dot_general x6, matrix products, full_pass(): jnp.einsum('qk,qd->kd', dscore, q_rows, preferred_element_type=jnp.float32)  11.7 us
    all_to_all x1, waiting for transfers between devices, body(): lax.all_to_all(own_k, 'uly', split_axis=0, concat_axis=1, tiled=True)  11.7 us
    all_to_all x1, waiting for transfers between devices, body(): lax.all_to_all(grad_out, 'uly', split_axis=1, concat_axis=0, tiled=True)  9.77 us
    all_to_all x1, waiting for transfers between devices, body(): lax.all_to_all(queries, 'uly', split_axis=1, concat_axis=0, tiled=True)  8.5 us
  transfers between devices with their start and end apart: 11, of which 7 were waited for; matrix products, arithmetic and copies ran while one was open for 7% of the time, Pallas kernels for 0%

commit v1 on v0

--- a/solution.py
+++ b/solution.py
@@ -17,7 +17,9 @@
 def body(queries, keys, values, grad_out, doc_start):
     q_all, k_all, v_all, d_all = (
         lax.all_to_all(queries, "uly", split_axis=1, concat_axis=0, tiled=True),
-        lax.all_to_all(keys, "uly", split_axis=1, concat_axis=0, tiled=True),
+        jnp.concatenate(
+            lax.all_to_all(jnp.stack(jnp.split(keys, lax.axis_size("uly"), 1)), "uly", 0, 0), 0
+        ),
         lax.all_to_all(values, "uly", split_axis=1, concat_axis=0, tiled=True),
         lax.all_to_all(grad_out, "uly", split_axis=1, concat_axis=0, tiled=True),
     )

time: 214 us -> 214 us (level)
  local copies, waits for them, and re-layouts: 20 us -> 29 us
  waiting for transfers between devices: 89.9 us -> 80.9 us
    unnamed x15 -> x30, local copies, waits for them, and re-layouts: 4.09 us -> 13.5 us
    all_to_all x1, waiting for transfers between devices: 13.3 us -> 4.26 us  [body(): lax.all_to_all(values, 'uly', split_axis=1, concat_axis=0, tiled=True)]
    all_to_all x1, starting transfers between devices: 7.52 us -> 4.16 us  [body(): lax.all_to_all(jnp.stack(jnp.split(keys, lax.axis_size('uly'), 1)), 'uly'...]
    all_to_all x1, starting transfers between devices: 4.16 us -> 7.52 us  [body(): lax.all_to_all(values, 'uly', split_axis=1, concat_axis=0, tiled=True)]
  transfers between devices with their start and end apart: 11 -> 11, of which waited for: 7 -> 7; matrix products, arithmetic and copies ran while one was open for 7% -> 11% of each run, Pallas kernels for 0% -> 0%
where the time goes in v1:
time: 214 us; the launch traced here: 212 us
  waiting for transfers between devices  80.9 us (38%)
  starting transfers between devices  43 us (20%)
  matrix products  41.5 us (19%)
  local copies, waits for them, and re-layouts  29 us (14%)
  other arithmetic  13.4 us (6%)
  loops' own time  3.49 us (2%)
    ppermute x4, waiting for transfers between devices, passed_along(): return lax.ppermute(array, axis, pairs)  33.3 us
    dot_general x12, matrix products, scores(): jnp.einsum('qd,kd->qk', q_rows, k_rows, preferred_element_type=jnp.float32)  15.9 us
    unnamed x30, local copies, waits for them, and re-layouts  13.5 us
    all_to_all x1, waiting for transfers between devices, body(): lax.all_to_all(jnp.stack(jnp.split(keys, lax.axis_size('uly'), 1)), 'uly'...  13.3 us
    dot_general x6, matrix products, full_pass(): jnp.einsum('qk,qd->kd', dscore, q_rows, preferred_element_type=jnp.float32)  11.7 us
    all_to_all x1, waiting for transfers between devices, body(): lax.all_to_all(own_k, 'uly', split_axis=0, concat_axis=1, tiled=True)  11.7 us
    all_to_all x1, waiting for transfers between devices, body(): lax.all_to_all(grad_out, 'uly', split_axis=1, concat_axis=0, tiled=True)  9.77 us
    all_to_all x1, waiting for transfers between devices, body(): lax.all_to_all(queries, 'uly', split_axis=1, concat_axis=0, tiled=True)  8.5 us
  transfers between devices with their start and end apart: 11, of which 7 were waited for; matrix products, arithmetic and copies ran while one was open for 11% of the time, Pallas kernels for 0%

profile of v1, /device:TPU:0, one launch (start us, length us, event | category | flops | bytes accessed | tf_op | source)
XLA Modules:
  0.0 212.2 jit_solution(16917816599556105300)
XLA Ops:
  2.6 7.5 %all-to-all-start.3 = ((bf16[128,16,128]{2,0,1:T(8,128)(2,1)}), bf16[128,16,128]{2,0,1:T(8,128)(2,1)S(1)}, u32[]{:S(2)}, u32[]{:S(2)}) async-start(bf16[128,16,128]{2,0,1:T(8,128)(2,1)} %copy_bitcast_fusion), calls=%async_computation.3 | async-start | bytes 1048576 | tf_op jit(solution)/shard_map/all_to_all | solution.py:23
  20.1 4.3 %all-to-all-done.3 = bf16[128,16,128]{2,0,1:T(8,128)(2,1)S(1)} async-done(((bf16[128,16,128]{2,0,1:T(8,128)(2,1)}), bf16[128,16,128]{2,0,1:T(8,128)(2,1)S(1)}, u32[]{:S(2)}, u32[]{:S(2)}) %all-to-all-start.3) | async-done | bytes 524320 | tf_op jit(solution)/shard_map/all_to_all | solution.py:23
  24.4 4.2 %all-to-all-start.2 = ((bf16[16,128,128]{2,1,0:T(8,128)(2,1)}), bf16[16,128,128]{2,1,0:T(8,128)(2,1)S(1)}, u32[]{:S(2)}, u32[]{:S(2)}) async-start(bf16[16,128,128]{2,1,0:T(8,128)(2,1)} %constant_dynamic-update-slice_fusion), calls=%async_computation.2 | async-start | bytes 1048576 | tf_op jit(solution)/shard_map/all_to_all | solution.py:21
  29.5 13.3 %all-to-all-done.2 = bf16[16,128,128]{2,1,0:T(8,128)(2,1)S(1)} async-done(((bf16[16,128,128]{2,1,0:T(8,128)(2,1)}), bf16[16,128,128]{2,1,0:T(8,128)(2,1)S(1)}, u32[]{:S(2)}, u32[]{:S(2)}) %all-to-all-start.2) | async-done | bytes 524320 | tf_op jit(solution)/shard_map/all_to_all | solution.py:21
  42.8 4.2 %all-to-all-start = ((bf16[128,16,128]{2,0,1:T(8,128)(2,1)}), bf16[128,16,128]{2,0,1:T(8,128)(2,1)S(1)}, u32[]{:S(2)}, u32[]{:S(2)}) async-start(bf16[128,16,128]{2,0,1:T(8,128)(2,1)} %copy_bitcast_fusion.2), calls=%async_computation | async-start | bytes 1048576 | tf_op jit(solution)/shard_map/all_to_all | solution.py:19
  48.0 3.4 %collective-permute-start.1 = (bf16[896,128]{1,0:T(8,128)(2,1)S(1)}, bf16[896,128]{1,0:T(8,128)(2,1)S(1)}, u32[]{:S(2)}, u32[]{:S(2)}) collective-permute-start(bf16[896,128]{1,0:T(8,128)(2,1)S(1)} %bitcast.146), channel_id=1, source_target_pairs={{0,16},{1,17},{2,18},{3,19},{4,20},{5,21},{6,22},{7,23},{8,24},{9,... | collective-permute-start | bytes 688136 | tf_op jit(solution)/shard_map/ppermute | solution.py:14
  51.5 1.3 collective-permute-start
  52.8 8.5 %all-to-all-done = bf16[128,16,128]{2,0,1:T(8,128)(2,1)S(1)} async-done(((bf16[128,16,128]{2,0,1:T(8,128)(2,1)}), bf16[128,16,128]{2,0,1:T(8,128)(2,1)S(1)}, u32[]{:S(2)}, u32[]{:S(2)}) %all-to-all-start) | async-done | bytes 524320 | tf_op jit(solution)/shard_map/all_to_all | solution.py:19
  61.3 4.2 %all-to-all-start.1 = ((bf16[128,16,128]{2,0,1:T(8,128)(2,1)}), bf16[128,16,128]{2,0,1:T(8,128)(2,1)}, u32[]{:S(2)}, u32[]{:S(2)}) async-start(bf16[128,16,128]{2,0,1:T(8,128)(2,1)} %copy_bitcast_fusion.1), calls=%async_computation.1 | async-start | bytes 1048576 | tf_op jit(solution)/shard_map/all_to_all | solution.py:24
  65.8 4.3 %pad_maximum_fusion.1 = (bf16[3072,128]{1,0:T(8,128)(2,1)S(1)}, bf16[3072,128]{1,0:T(8,128)(2,1)}) fusion(bf16[2048,128]{1,0:T(8,128)(2,1)S(1)} %bitcast.139, bf16[896,128]{1,0:T(8,128)(2,1)S(1)} %collective-permute-done.1, bf16[3072]{0:T(1024)(128)(2,1)S(1)} %pad.8.clone, bf16[2048,128]{1,0:T(8,128)(2,1)S(1)} %bitcast.140, ...), kind=kLoop, calls=%fused_computation.48 | loop fusion | flops 4325376 | bytes 3086336 | tf_op jit(solution)/shard_map/concatenate | solution.py:43
  70.1 9.8 %all-to-all-done.1 = bf16[128,16,128]{2,0,1:T(8,128)(2,1)} async-done(((bf16[128,16,128]{2,0,1:T(8,128)(2,1)}), bf16[128,16,128]{2,0,1:T(8,128)(2,1)}, u32[]{:S(2)}, u32[]{:S(2)}) %all-to-all-start.1) | async-done | bytes 524320 | tf_op jit(solution)/shard_map/all_to_all | solution.py:24
  82.1 58.6 %while.115 = (s32[]{:T(128)}, bf16[2048,128]{1,0:T(8,128)(2,1)}, f32[3072,128]{1,0:T(8,128)}, f32[3072,128]{1,0:T(8,128)S(1)}, s32[2048]{0:T(1024)S(1)}, /*index...) while((s32[]{:T(128)}, bf16[2048,128]{1,0:T(8,128)(2,1)}, ...), condition=%wide.region_8.9_spmd.clone.clone, body=%wide.region_0.8_spmd.clone.clone.sunk | while | flops 478156288 | bytes 12199279 | solution.py:144
  84.5 2.3 %while.116 = (s32[]{:T(128)}, f32[512]{0:T(512)S(1)}, f32[512]{0:T(512)S(1)}, f32[512]{0:T(512)S(1)}, s32[]{:T(128)}, /*index=5*/s32[512]{0:T(512)S(1)}, s32[307...) while((s32[]{:T(128)}, f32[512]{0:T(512)S(1)}, ...), condition=%wide.region_5.5_spmd, body=%wide.region_1.4_spmd.sunk | while | flops 139200000 | bytes 3739867 | solution.py:96
  84.7 1.3 fusion.69
  86.8 5.4 %while.117 = (s32[]{:T(128)}, f32[512,128]{1,0:T(8,128)S(1)}, f32[3072,128]{1,0:T(8,128)}, f32[3072,128]{1,0:T(8,128)S(1)}, s32[]{:T(128)}, /*index=5*/s32[512]{...) while((s32[]{:T(128)}, f32[512,128]{1,0:T(8,128)S(1)}, ...), condition=%wide.region_7.7_spmd, body=%wide.region_6.6_spmd.sunk | while | flops 338886656 | bytes 7229687 | solution.py:131
  87.0 1.4 fusion.82
  90.3 1.9 fusion.84
  95.4 4.5 %while.116 = (s32[]{:T(128)}, f32[512]{0:T(512)S(1)}, f32[512]{0:T(512)S(1)}, f32[512]{0:T(512)S(1)}, s32[]{:T(128)}, /*index=5*/s32[512]{0:T(512)S(1)}, s32[307...) while((s32[]{:T(128)}, f32[512]{0:T(512)S(1)}, ...), condition=%wide.region_5.5_spmd, body=%wide.region_1.4_spmd.sunk | while | flops 139200000 | bytes 3739867 | solution.py:96
  95.5 1.3 fusion.69
  97.8 1.3 fusion.69
  100.0 10.8 %while.117 = (s32[]{:T(128)}, f32[512,128]{1,0:T(8,128)S(1)}, f32[3072,128]{1,0:T(8,128)}, f32[3072,128]{1,0:T(8,128)S(1)}, s32[]{:T(128)}, /*index=5*/s32[512]{...) while((s32[]{:T(128)}, f32[512,128]{1,0:T(8,128)S(1)}, ...), condition=%wide.region_7.7_spmd, body=%wide.region_6.6_spmd.sunk | while | flops 338886656 | bytes 7229687 | solution.py:131
  100.1 1.4 fusion.82
  101.8 1.3 convolution_add_fusion.4
  103.4 1.9 fusion.84
  105.5 1.4 fusion.82
  108.8 2.0 fusion.84
  113.8 2.3 %while.116 = (s32[]{:T(128)}, f32[512]{0:T(512)S(1)}, f32[512]{0:T(512)S(1)}, f32[512]{0:T(512)S(1)}, s32[]{:T(128)}, /*index=5*/s32[512]{0:T(512)S(1)}, s32[307...) while((s32[]{:T(128)}, f32[512]{0:T(512)S(1)}, ...), condition=%wide.region_5.5_spmd, body=%wide.region_1.4_spmd.sunk | while | flops 139200000 | bytes 3739867 | solution.py:96
  114.0 1.3 fusion.69
  116.1 5.4 %while.117 = (s32[]{:T(128)}, f32[512,128]{1,0:T(8,128)S(1)}, f32[3072,128]{1,0:T(8,128)}, f32[3072,128]{1,0:T(8,128)S(1)}, s32[]{:T(128)}, /*index=5*/s32[512]{...) while((s32[]{:T(128)}, f32[512,128]{1,0:T(8,128)S(1)}, ...), condition=%wide.region_7.7_spmd, body=%wide.region_6.6_spmd.sunk | while | flops 338886656 | bytes 7229687 | solution.py:131
  116.3 1.4 fusion.82
  119.6 1.9 fusion.84
  124.6 4.5 %while.116 = (s32[]{:T(128)}, f32[512]{0:T(512)S(1)}, f32[512]{0:T(512)S(1)}, f32[512]{0:T(512)S(1)}, s32[]{:T(128)}, /*index=5*/s32[512]{0:T(512)S(1)}, s32[307...) while((s32[]{:T(128)}, f32[512]{0:T(512)S(1)}, ...), condition=%wide.region_5.5_spmd, body=%wide.region_1.4_spmd.sunk | while | flops 139200000 | bytes 3739867 | solution.py:96
  124.8 1.3 fusion.69
  127.1 1.3 fusion.69
  129.2 10.8 %while.117 = (s32[]{:T(128)}, f32[512,128]{1,0:T(8,128)S(1)}, f32[3072,128]{1,0:T(8,128)}, f32[3072,128]{1,0:T(8,128)S(1)}, s32[]{:T(128)}, /*index=5*/s32[512]{...) while((s32[]{:T(128)}, f32[512,128]{1,0:T(8,128)S(1)}, ...), condition=%wide.region_7.7_spmd, body=%wide.region_6.6_spmd.sunk | while | flops 338886656 | bytes 7229687 | solution.py:131
  129.4 1.4 fusion.82
  132.7 1.9 fusion.84
  134.8 1.4 fusion.82
  138.0 1.9 fusion.84
  140.7 4.2 %all-to-all-start.4 = ((bf16[16,128,128]{2,1,0:T(8,128)(2,1)}), bf16[16,128,128]{2,1,0:T(8,128)(2,1)S(1)}, u32[]{:S(2)}, u32[]{:S(2)}) async-start(bf16[16,128,128]{2,1,0:T(8,128)(2,1)} %bitcast.142), calls=%async_computation.4 | async-start | bytes 1048576 | tf_op jit(solution)/shard_map/all_to_all | solution.py:158
  144.9 1.3 collective-permute-start.3
  146.3 22.9 %collective-permute-done.3 = bf16[896,128]{1,0:T(8,128)(2,1)S(1)} collective-permute-done((bf16[896,128]{1,0:T(8,128)(2,1)S(1)}, bf16[896,128]{1,0:T(8,128)(2,1)S(1)}, u32[]{:S(2)}, u32[]{:S(2)}) %collective-permute-start.3) | collective-permute-done | bytes 229408 | tf_op jit(solution)/shard_map/ppermute | solution.py:14
  170.1 5.7 %all-to-all-start.6 = ((bf16[16,128,128]{2,1,0:T(8,128)(2,1)}), bf16[16,128,128]{2,1,0:T(8,128)(2,1)S(1)}, u32[]{:S(2)}, u32[]{:S(2)}) async-start(bf16[16,128,128]{2,1,0:T(8,128)(2,1)} %bitcast.36), calls=%async_computation.6 | async-start | bytes 1048576 | tf_op jit(solution)/shard_map/all_to_all | solution.py:160
  175.8 1.5 convert.16
  177.3 1.3 collective-permute-start.2
  178.6 10.4 %collective-permute-done.2 = bf16[896,128]{1,0:T(8,128)(2,1)S(1)} collective-permute-done((bf16[896,128]{1,0:T(8,128)(2,1)S(1)}, bf16[896,128]{1,0:T(8,128)(2,1)S(1)}, u32[]{:S(2)}, u32[]{:S(2)}) %collective-permute-start.2) | collective-permute-done | bytes 229408 | tf_op jit(solution)/shard_map/ppermute | solution.py:14
  190.9 5.7 %all-to-all-start.5 = ((bf16[16,128,128]{2,1,0:T(8,128)(2,1)}), bf16[16,128,128]{2,1,0:T(8,128)(2,1)S(1)}, u32[]{:S(2)}, u32[]{:S(2)}) async-start(bf16[16,128,128]{2,1,0:T(8,128)(2,1)} %bitcast.33), calls=%async_computation.5 | async-start | bytes 1048576 | tf_op jit(solution)/shard_map/all_to_all | solution.py:159
  199.2 11.7 %all-to-all-done.5 = bf16[16,128,128]{2,1,0:T(8,128)(2,1)S(1)} async-done(((bf16[16,128,128]{2,1,0:T(8,128)(2,1)}), bf16[16,128,128]{2,1,0:T(8,128)(2,1)S(1)}, u32[]{:S(2)}, u32[]{:S(2)}) %all-to-all-start.5) | async-done | bytes 524320 | tf_op jit(solution)/shard_map/all_to_all | solution.py:159
  (180 shorter events, 49.4 us)
Async XLA Ops:
  0.6 1.0 copy-start
  0.6 9.5 %copy-start.2 = (bf16[128,2048]{1,0:T(8,128)(2,1)S(1)}, bf16[128,2048]{1,0:T(8,128)(2,1)}, u32[]{:S(2)}) copy-start(bf16[128,2048]{1,0:T(8,128)(2,1)} %param.12) | copy-start | bytes 1572868
  2.6 26.0 %copy-start.3 = (bf16[128,2048]{1,0:T(8,128)(2,1)S(1)}, bf16[128,2048]{1,0:T(8,128)(2,1)}, u32[]{:S(2)}) copy-start(bf16[128,2048]{1,0:T(8,128)(2,1)} %param.11) | copy-start | bytes 1572868
  2.6 21.8 %all-to-all-start.3 = ((bf16[128,16,128]{2,0,1:T(8,128)(2,1)}), bf16[128,16,128]{2,0,1:T(8,128)(2,1)S(1)}, u32[]{:S(2)}, u32[]{:S(2)}) async-start(bf16[128,16,128]{2,0,1:T(8,128)(2,1)} %copy_bitcast_fusion), calls=%async_computation.3 | async-start | bytes 1048576 | tf_op jit(solution)/shard_map/all_to_all | solution.py:23
  20.1 26.9 %copy-start.4 = (bf16[128,2048]{1,0:T(8,128)(2,1)S(1)}, bf16[128,2048]{1,0:T(8,128)(2,1)}, u32[]{:S(2)}) copy-start(bf16[128,2048]{1,0:T(8,128)(2,1)} %param.14) | copy-start | bytes 1572868
  24.4 18.4 %all-to-all-start.2 = ((bf16[16,128,128]{2,1,0:T(8,128)(2,1)}), bf16[16,128,128]{2,1,0:T(8,128)(2,1)S(1)}, u32[]{:S(2)}, u32[]{:S(2)}) async-start(bf16[16,128,128]{2,1,0:T(8,128)(2,1)} %constant_dynamic-update-slice_fusion), calls=%async_computation.2 | async-start | bytes 1048576 | tf_op jit(solution)/shard_map/all_to_all | solution.py:21
  42.8 18.4 %all-to-all-start = ((bf16[128,16,128]{2,0,1:T(8,128)(2,1)}), bf16[128,16,128]{2,0,1:T(8,128)(2,1)S(1)}, u32[]{:S(2)}, u32[]{:S(2)}) async-start(bf16[128,16,128]{2,0,1:T(8,128)(2,1)} %copy_bitcast_fusion.2), calls=%async_computation | async-start | bytes 1048576 | tf_op jit(solution)/shard_map/all_to_all | solution.py:19
  47.0 18.5 %copy-start.5 = (s32[32]{0:T(128)S(1)}, s32[32]{0:T(128)}, u32[]{:S(2)}) copy-start(s32[32]{0:T(128)} %param.15) | copy-start | bytes 388
  48.0 17.8 %collective-permute-start.1 = (bf16[896,128]{1,0:T(8,128)(2,1)S(1)}, bf16[896,128]{1,0:T(8,128)(2,1)S(1)}, u32[]{:S(2)}, u32[]{:S(2)}) collective-permute-start(bf16[896,128]{1,0:T(8,128)(2,1)S(1)} %bitcast.146), channel_id=1, source_target_pairs={{0,16},{1,17},{2,18},{3,19},{4,20},{5,21},{6,22},{7,23},{8,24},{9,... | collective-permute-start | bytes 688136 | tf_op jit(solution)/shard_map/ppermute | solution.py:14
  51.5 14.3 %collective-permute-start = (bf16[896,128]{1,0:T(8,128)(2,1)S(1)}, bf16[896,128]{1,0:T(8,128)(2,1)S(1)}, u32[]{:S(2)}, u32[]{:S(2)}) collective-permute-start(bf16[896,128]{1,0:T(8,128)(2,1)S(1)} %bitcast.147), channel_id=1, source_target_pairs={{0,16},{1,17},{2,18},{3,19},{4,20},{5,21},{6,22},{7,23},{8,24},{9,... | collective-permute-start | bytes 688136 | tf_op jit(solution)/shard_map/ppermute | solution.py:14
  61.3 8.8 %copy-start.1 = (bf16[128,16,128]{2,0,1:T(8,128)(2,1)}, bf16[128,16,128]{2,0,1:T(8,128)(2,1)S(1)}, u32[]{:S(2)}) copy-start(bf16[128,16,128]{2,0,1:T(8,128)(2,1)S(1)} %all-to-all-done) | copy-start | bytes 1572868
  61.3 18.5 %all-to-all-start.1 = ((bf16[128,16,128]{2,0,1:T(8,128)(2,1)}), bf16[128,16,128]{2,0,1:T(8,128)(2,1)}, u32[]{:S(2)}, u32[]{:S(2)}) async-start(bf16[128,16,128]{2,0,1:T(8,128)(2,1)} %copy_bitcast_fusion.1), calls=%async_computation.1 | async-start | bytes 1048576 | tf_op jit(solution)/shard_map/all_to_all | solution.py:24
  140.7 29.4 %all-to-all-start.4 = ((bf16[16,128,128]{2,1,0:T(8,128)(2,1)}), bf16[16,128,128]{2,1,0:T(8,128)(2,1)S(1)}, u32[]{:S(2)}, u32[]{:S(2)}) async-start(bf16[16,128,128]{2,1,0:T(8,128)(2,1)} %bitcast.142), calls=%async_computation.4 | async-start | bytes 1048576 | tf_op jit(solution)/shard_map/all_to_all | solution.py:158
  144.9 24.2 %collective-permute-start.3 = (bf16[896,128]{1,0:T(8,128)(2,1)S(1)}, bf16[896,128]{1,0:T(8,128)(2,1)S(1)}, u32[]{:S(2)}, u32[]{:S(2)}) collective-permute-start(bf16[896,128]{1,0:T(8,128)(2,1)S(1)} %slice.80), channel_id=1, source_target_pairs={{16,0},{17,1},{18,2},{19,3},{20,4},{21,5},{22,6},{23,7},{24,8},{25... | collective-permute-start | bytes 688136 | tf_op jit(solution)/shard_map/ppermute | solution.py:14
  170.1 20.9 %all-to-all-start.6 = ((bf16[16,128,128]{2,1,0:T(8,128)(2,1)}), bf16[16,128,128]{2,1,0:T(8,128)(2,1)S(1)}, u32[]{:S(2)}, u32[]{:S(2)}) async-start(bf16[16,128,128]{2,1,0:T(8,128)(2,1)} %bitcast.36), calls=%async_computation.6 | async-start | bytes 1048576 | tf_op jit(solution)/shard_map/all_to_all | solution.py:160
  177.3 11.7 %collective-permute-start.2 = (bf16[896,128]{1,0:T(8,128)(2,1)S(1)}, bf16[896,128]{1,0:T(8,128)(2,1)S(1)}, u32[]{:S(2)}, u32[]{:S(2)}) collective-permute-start(bf16[896,128]{1,0:T(8,128)(2,1)S(1)} %slice.78), channel_id=1, source_target_pairs={{16,0},{17,1},{18,2},{19,3},{20,4},{21,5},{22,6},{23,7},{24,8},{25... | collective-permute-start | bytes 688136 | tf_op jit(solution)/shard_map/ppermute | solution.py:14
  190.9 20.0 %all-to-all-start.5 = ((bf16[16,128,128]{2,1,0:T(8,128)(2,1)}), bf16[16,128,128]{2,1,0:T(8,128)(2,1)S(1)}, u32[]{:S(2)}, u32[]{:S(2)}) async-start(bf16[16,128,128]{2,1,0:T(8,128)(2,1)} %bitcast.33), calls=%async_computation.5 | async-start | bytes 1048576 | tf_op jit(solution)/shard_map/all_to_all | solution.py:159
